TPU v7x, 32 devices: a whole 2x2x4 slice. The times are simulated.
32 devices in a mesh: win: 4 (over z), sec: 8 (over y, x, core).
Axes of the slice: x: 2, y: 2, z: 4, core: 2. Of those that a mesh axis runs over, the one named last changes fastest.
Arguments:
- initial: bfloat16 [5, 8, 24, 512], P(None, 'win'), may hold values from -6 to 6
- props: bfloat16 [8, 8, 2, 256, 256], P('sec'), may hold values from -0.25 to 0.25
- screen: float32 [8, 8, 256], P('sec', 'win'), may hold values from -3.140625 to 3.140625
- links: int32 [8, 8, 6], P('sec', 'win'), may hold values from 0 to 7, as said below
- kinds: int32 [8, 8, 6], P('sec', 'win'), may hold values from 0 to 7
- counts: int32 [8, 8], P('sec', 'win'), may hold values from 1 to 6
Outputs:
- fields: bfloat16 [8, 5, 8, 24, 512], P('sec', None, 'win')
Inputs may be any that keep to these rules, and one draw needn't show every extreme that they name: links[s, w, l] lies within w - 1 to w + 1.
All inputs are finite; a program needn't handle non-finite values.
Results may differ from a plain program's by a relative error of at most 0.033.
Values may be sent and summed in bfloat16 or wider, within the bound.
A program may use at most 64 MiB of HBM per device.

v0:
```python
import jax
import jax.numpy as jnp
from jax import lax
from jax.sharding import PartitionSpec as P


def with_halo(block, sides, width):
    for axis, dim in sides:
        count = lax.axis_size(axis)
        forward = [(i, i + 1) for i in range(count - 1)]
        backward = [(target, source) for source, target in forward]
        low = lax.ppermute(
            lax.slice_in_dim(block, block.shape[dim] - width, None, axis=dim), axis, forward
        )
        high = lax.ppermute(lax.slice_in_dim(block, 0, width, axis=dim), axis, backward)
        block = jnp.concatenate([low, block, high], axis=dim)
    return block


def shifted(array, axis, by):
    count = lax.axis_size(axis)
    pairs = [(i, i + by) for i in range(count) if 0 <= i + by < count]
    return lax.ppermute(array, axis, pairs)


def local(initial, props, screen, links, kinds, counts):
    coeffs = props.shape[-1]
    entries = props.shape[1]
    section_table = props[0]
    real_part = section_table[:, 0]
    imag_part = section_table[:, 1]
    upper = jnp.concatenate([real_part, imag_part], axis=-1)
    lower = jnp.concatenate([-imag_part, real_part], axis=-1)
    blocks = jnp.concatenate([upper, lower], axis=-2)
    local_windows = links.shape[1]
    list_length = links.shape[2]
    first_window = lax.axis_index("win") * local_windows
    position = first_window - 1 + jnp.arange(local_windows + 2, dtype=jnp.int32)
    count_rows = counts[0]
    weighting = (jnp.arange(list_length)[None, :] < count_rows[:, None]).astype(jnp.float32)
    weighting = weighting * lax.rsqrt(count_rows.astype(jnp.float32))[:, None]
    source_hit = (links[0][:, :, None] == position[None, None, :]).astype(jnp.float32)
    kind_hit = (kinds[0][:, :, None] == jnp.arange(entries)[None, None, :]).astype(jnp.float32)
    selection = jnp.einsum(
        "wl,wlj,wlp->pwj", weighting, source_hit, kind_hit, precision=lax.Precision.HIGHEST
    )
    screen_phase = screen[0]
    cosine = jnp.cos(screen_phase)[None, :, None, :]
    sine_part = jnp.sin(screen_phase)[None, :, None, :]

    def advance(padded):
        batch_count = padded.shape[0]
        flat_rows = padded.reshape(-1, 2 * coeffs)
        total = jnp.zeros((batch_count, local_windows) + padded.shape[2:], jnp.float32)
        for entry in range(entries):
            product = jnp.dot(flat_rows, blocks[entry], preferred_element_type=jnp.float32).reshape(
                padded.shape
            )
            total = total + jnp.einsum(
                "wj,bjsd->bwsd", selection[entry], product, precision=lax.Precision.HIGHEST
            )
        real_out = total[..., :coeffs]
        imag_out = total[..., coeffs:]
        return jnp.concatenate(
            [real_out * cosine - imag_out * sine_part, real_out * sine_part + imag_out * cosine],
            axis=-1,
        ).astype(jnp.bfloat16)

    section_index = lax.axis_index("sec")
    sections = lax.axis_size("sec")
    fronts = initial.shape[0]

    def tick_step(tick_index, carry):
        received, outputs = carry
        front_index = tick_index - section_index
        active = (front_index >= 0) & (front_index < fronts)
        front_slot = jnp.clip(front_index, 0, fronts - 1)
        entering = lax.dynamic_slice_in_dim(initial, front_slot, 1, 0)
        incoming = jnp.where(section_index == 0, entering, received)
        padded = with_halo(incoming, (("win", 1),), 1)
        advanced = lax.cond(active, advance, lambda unused: jnp.zeros_like(received), padded)
        updated = lax.dynamic_update_slice_in_dim(outputs, advanced, front_slot, 0)
        outputs = jnp.where(active, updated, outputs)
        received = shifted(advanced, "sec", 1)
        return (received, outputs)

    empty_front = jnp.zeros_like(initial[:1])
    final_in, outputs = lax.fori_loop(
        0, sections + fronts - 1, tick_step, (empty_front, jnp.zeros_like(initial))
    )
    return outputs[None]


def solution(mesh):
    placed = (
        P(None, "win", None, None),
        P("sec", None, None, None, None),
        P("sec", "win", None),
        P("sec", "win", None),
        P("sec", "win", None),
        P("sec", "win"),
    )
    return jax.shard_map(
        local,
        mesh=mesh,
        in_specs=placed,
        out_specs=P("sec", None, "win", None, None),
        check_vma=False,
    )
```

profile of v0, /device:TPU:7, one launch (start us, length us, event | category | flops | bytes accessed | tf_op | source)
XLA Modules:
  0.0 278.4 jit_solution(1189030397635785630)
XLA Ops:
  4.9 272.8 %while.16 = (s32[]{:T(128)}, bf16[1,2,24,512]{3,1,2,0:T(2,128)(2,1)S(1)}, bf16[5,2,24,512]{3,2,1,0:T(8,128)(2,1)S(1)}, s32[]{:T(128)}, pred[]{:T(512)}, /*index=...) while((s32[]{:T(128)}, ...), condition=%wide.region_3.4_spmd, body=%wide.region_0.3_spmd.sunk | while | flops 412606464 | bytes 28307860 | solution.py:88
  17.1 4.6 %collective-permute-start.1 = (bf16[1,1,24,512]{3,2,1,0:T(8,128)(2,1)S(1)}, bf16[1,1,24,512]{3,2,1,0:T(8,128)(2,1)S(1)}, u32[]{:S(2)}, u32[]{:S(2)}) collective-permute-start(bf16[1,1,24,512]{3,2,1,0:T(8,128)(2,1)S(1)} %get-tuple-element.326), channel_id=1, source_target_pairs={{0,8},{8,16},{16,24},{1,9},{9,17},{17,25},{2,10},{10,18},{18,26},{... | collective-permute-start | bytes 73736 | tf_op jit(solution)/shard_map/while/body/eval_jaxpr/ppermute | solution.py:12
  24.1 4.9 %collective-permute-done.2 = bf16[1,2,24,512]{3,1,2,0:T(2,128)(2,1)S(1)} collective-permute-done((bf16[1,2,24,512]{3,1,2,0:T(2,128)(2,1)S(1)}, bf16[1,2,24,512]{3,1,2,0:T(2,128)(2,1)S(1)}, u32[]{:S(2)}, u32[]{:S(2)}) %collective-permute-start.2) | collective-permute-done | bytes 49184 | tf_op jit(solution)/shard_map/while/body/eval_jaxpr/ppermute | solution.py:23
  30.3 4.6 %collective-permute-start.1 = (bf16[1,1,24,512]{3,2,1,0:T(8,128)(2,1)S(1)}, bf16[1,1,24,512]{3,2,1,0:T(8,128)(2,1)S(1)}, u32[]{:S(2)}, u32[]{:S(2)}) collective-permute-start(bf16[1,1,24,512]{3,2,1,0:T(8,128)(2,1)S(1)} %get-tuple-element.326), channel_id=1, source_target_pairs={{0,8},{8,16},{16,24},{1,9},{9,17},{17,25},{2,10},{10,18},{18,26},{... | collective-permute-start | bytes 73736 | tf_op jit(solution)/shard_map/while/body/eval_jaxpr/ppermute | solution.py:12
  37.3 4.9 %collective-permute-done.2 = bf16[1,2,24,512]{3,1,2,0:T(2,128)(2,1)S(1)} collective-permute-done((bf16[1,2,24,512]{3,1,2,0:T(2,128)(2,1)S(1)}, bf16[1,2,24,512]{3,1,2,0:T(2,128)(2,1)S(1)}, u32[]{:S(2)}, u32[]{:S(2)}) %collective-permute-start.2) | collective-permute-done | bytes 49184 | tf_op jit(solution)/shard_map/while/body/eval_jaxpr/ppermute | solution.py:23
  43.5 4.6 %collective-permute-start.1 = (bf16[1,1,24,512]{3,2,1,0:T(8,128)(2,1)S(1)}, bf16[1,1,24,512]{3,2,1,0:T(8,128)(2,1)S(1)}, u32[]{:S(2)}, u32[]{:S(2)}) collective-permute-start(bf16[1,1,24,512]{3,2,1,0:T(8,128)(2,1)S(1)} %get-tuple-element.326), channel_id=1, source_target_pairs={{0,8},{8,16},{16,24},{1,9},{9,17},{17,25},{2,10},{10,18},{18,26},{... | collective-permute-start | bytes 73736 | tf_op jit(solution)/shard_map/while/body/eval_jaxpr/ppermute | solution.py:12
  50.5 4.9 %collective-permute-done.2 = bf16[1,2,24,512]{3,1,2,0:T(2,128)(2,1)S(1)} collective-permute-done((bf16[1,2,24,512]{3,1,2,0:T(2,128)(2,1)S(1)}, bf16[1,2,24,512]{3,1,2,0:T(2,128)(2,1)S(1)}, u32[]{:S(2)}, u32[]{:S(2)}) %collective-permute-start.2) | collective-permute-done | bytes 49184 | tf_op jit(solution)/shard_map/while/body/eval_jaxpr/ppermute | solution.py:23
  56.7 4.6 %collective-permute-start.1 = (bf16[1,1,24,512]{3,2,1,0:T(8,128)(2,1)S(1)}, bf16[1,1,24,512]{3,2,1,0:T(8,128)(2,1)S(1)}, u32[]{:S(2)}, u32[]{:S(2)}) collective-permute-start(bf16[1,1,24,512]{3,2,1,0:T(8,128)(2,1)S(1)} %get-tuple-element.326), channel_id=1, source_target_pairs={{0,8},{8,16},{16,24},{1,9},{9,17},{17,25},{2,10},{10,18},{18,26},{... | collective-permute-start | bytes 73736 | tf_op jit(solution)/shard_map/while/body/eval_jaxpr/ppermute | solution.py:12
  63.7 4.9 %collective-permute-done.2 = bf16[1,2,24,512]{3,1,2,0:T(2,128)(2,1)S(1)} collective-permute-done((bf16[1,2,24,512]{3,1,2,0:T(2,128)(2,1)S(1)}, bf16[1,2,24,512]{3,1,2,0:T(2,128)(2,1)S(1)}, u32[]{:S(2)}, u32[]{:S(2)}) %collective-permute-start.2) | collective-permute-done | bytes 49184 | tf_op jit(solution)/shard_map/while/body/eval_jaxpr/ppermute | solution.py:23
  69.9 4.6 %collective-permute-start.1 = (bf16[1,1,24,512]{3,2,1,0:T(8,128)(2,1)S(1)}, bf16[1,1,24,512]{3,2,1,0:T(8,128)(2,1)S(1)}, u32[]{:S(2)}, u32[]{:S(2)}) collective-permute-start(bf16[1,1,24,512]{3,2,1,0:T(8,128)(2,1)S(1)} %get-tuple-element.326), channel_id=1, source_target_pairs={{0,8},{8,16},{16,24},{1,9},{9,17},{17,25},{2,10},{10,18},{18,26},{... | collective-permute-start | bytes 73736 | tf_op jit(solution)/shard_map/while/body/eval_jaxpr/ppermute | solution.py:12
  76.9 4.9 %collective-permute-done.2 = bf16[1,2,24,512]{3,1,2,0:T(2,128)(2,1)S(1)} collective-permute-done((bf16[1,2,24,512]{3,1,2,0:T(2,128)(2,1)S(1)}, bf16[1,2,24,512]{3,1,2,0:T(2,128)(2,1)S(1)}, u32[]{:S(2)}, u32[]{:S(2)}) %collective-permute-start.2) | collective-permute-done | bytes 49184 | tf_op jit(solution)/shard_map/while/body/eval_jaxpr/ppermute | solution.py:23
  83.2 4.6 %collective-permute-start.1 = (bf16[1,1,24,512]{3,2,1,0:T(8,128)(2,1)S(1)}, bf16[1,1,24,512]{3,2,1,0:T(8,128)(2,1)S(1)}, u32[]{:S(2)}, u32[]{:S(2)}) collective-permute-start(bf16[1,1,24,512]{3,2,1,0:T(8,128)(2,1)S(1)} %get-tuple-element.326), channel_id=1, source_target_pairs={{0,8},{8,16},{16,24},{1,9},{9,17},{17,25},{2,10},{10,18},{18,26},{... | collective-permute-start | bytes 73736 | tf_op jit(solution)/shard_map/while/body/eval_jaxpr/ppermute | solution.py:12
  90.1 66.3 %collective-permute-done.2 = bf16[1,2,24,512]{3,1,2,0:T(2,128)(2,1)S(1)} collective-permute-done((bf16[1,2,24,512]{3,1,2,0:T(2,128)(2,1)S(1)}, bf16[1,2,24,512]{3,1,2,0:T(2,128)(2,1)S(1)}, u32[]{:S(2)}, u32[]{:S(2)}) %collective-permute-start.2) | collective-permute-done | bytes 49184 | tf_op jit(solution)/shard_map/while/body/eval_jaxpr/ppermute | solution.py:23
  157.8 4.6 %collective-permute-start.1 = (bf16[1,1,24,512]{3,2,1,0:T(8,128)(2,1)S(1)}, bf16[1,1,24,512]{3,2,1,0:T(8,128)(2,1)S(1)}, u32[]{:S(2)}, u32[]{:S(2)}) collective-permute-start(bf16[1,1,24,512]{3,2,1,0:T(8,128)(2,1)S(1)} %get-tuple-element.326), channel_id=1, source_target_pairs={{0,8},{8,16},{16,24},{1,9},{9,17},{17,25},{2,10},{10,18},{18,26},{... | collective-permute-start | bytes 73736 | tf_op jit(solution)/shard_map/while/body/eval_jaxpr/ppermute | solution.py:12
  163.3 11.0 %conditional.2 = (bf16[1,2,24,512]{3,1,2,0:T(2,128)(2,1)S(1)}) conditional(s32[]{:T(128)} %convert_element_type.30, () %tuple.47, (bf16[1,4,24,512]{3,2,1,0:T(8,128)(2,1)S(1)}, bf16[8,512,512]{2,1,0:T(8,128)(2,1)}, f32[8,2,4]{2,1,0:T(2,128)S(1)}, f32[1,2,1,256]{3,1,2,0:T(2,128)S(1)}, f32[1,2,1,256]{3,1,2,0:T(2,128)S(1)}) %tuple.48), branch_computations={%region_1.1_spmd, %region_2.2_spmd} | conditional | flops 412459008 | bytes 26636324 | solution.py:81
  175.7 5.8 %collective-permute-done.2 = bf16[1,2,24,512]{3,1,2,0:T(2,128)(2,1)S(1)} collective-permute-done((bf16[1,2,24,512]{3,1,2,0:T(2,128)(2,1)S(1)}, bf16[1,2,24,512]{3,1,2,0:T(2,128)(2,1)S(1)}, u32[]{:S(2)}, u32[]{:S(2)}) %collective-permute-start.2) | collective-permute-done | bytes 49184 | tf_op jit(solution)/shard_map/while/body/eval_jaxpr/ppermute | solution.py:23
  182.9 4.6 %collective-permute-start.1 = (bf16[1,1,24,512]{3,2,1,0:T(8,128)(2,1)S(1)}, bf16[1,1,24,512]{3,2,1,0:T(8,128)(2,1)S(1)}, u32[]{:S(2)}, u32[]{:S(2)}) collective-permute-start(bf16[1,1,24,512]{3,2,1,0:T(8,128)(2,1)S(1)} %get-tuple-element.326), channel_id=1, source_target_pairs={{0,8},{8,16},{16,24},{1,9},{9,17},{17,25},{2,10},{10,18},{18,26},{... | collective-permute-start | bytes 73736 | tf_op jit(solution)/shard_map/while/body/eval_jaxpr/ppermute | solution.py:12
  188.4 11.0 %conditional.2 = (bf16[1,2,24,512]{3,1,2,0:T(2,128)(2,1)S(1)}) conditional(s32[]{:T(128)} %convert_element_type.30, () %tuple.47, (bf16[1,4,24,512]{3,2,1,0:T(8,128)(2,1)S(1)}, bf16[8,512,512]{2,1,0:T(8,128)(2,1)}, f32[8,2,4]{2,1,0:T(2,128)S(1)}, f32[1,2,1,256]{3,1,2,0:T(2,128)S(1)}, f32[1,2,1,256]{3,1,2,0:T(2,128)S(1)}) %tuple.48), branch_computations={%region_1.1_spmd, %region_2.2_spmd} | conditional | flops 412459008 | bytes 26636324 | solution.py:81
  200.8 5.8 %collective-permute-done.2 = bf16[1,2,24,512]{3,1,2,0:T(2,128)(2,1)S(1)} collective-permute-done((bf16[1,2,24,512]{3,1,2,0:T(2,128)(2,1)S(1)}, bf16[1,2,24,512]{3,1,2,0:T(2,128)(2,1)S(1)}, u32[]{:S(2)}, u32[]{:S(2)}) %collective-permute-start.2) | collective-permute-done | bytes 49184 | tf_op jit(solution)/shard_map/while/body/eval_jaxpr/ppermute | solution.py:23
  213.5 11.0 %conditional.2 = (bf16[1,2,24,512]{3,1,2,0:T(2,128)(2,1)S(1)}) conditional(s32[]{:T(128)} %convert_element_type.30, () %tuple.47, (bf16[1,4,24,512]{3,2,1,0:T(8,128)(2,1)S(1)}, bf16[8,512,512]{2,1,0:T(8,128)(2,1)}, f32[8,2,4]{2,1,0:T(2,128)S(1)}, f32[1,2,1,256]{3,1,2,0:T(2,128)S(1)}, f32[1,2,1,256]{3,1,2,0:T(2,128)S(1)}) %tuple.48), branch_computations={%region_1.1_spmd, %region_2.2_spmd} | conditional | flops 412459008 | bytes 26636324 | solution.py:81
  225.9 5.8 %collective-permute-done.2 = bf16[1,2,24,512]{3,1,2,0:T(2,128)(2,1)S(1)} collective-permute-done((bf16[1,2,24,512]{3,1,2,0:T(2,128)(2,1)S(1)}, bf16[1,2,24,512]{3,1,2,0:T(2,128)(2,1)S(1)}, u32[]{:S(2)}, u32[]{:S(2)}) %collective-permute-start.2) | collective-permute-done | bytes 49184 | tf_op jit(solution)/shard_map/while/body/eval_jaxpr/ppermute | solution.py:23
  238.5 11.0 %conditional.2 = (bf16[1,2,24,512]{3,1,2,0:T(2,128)(2,1)S(1)}) conditional(s32[]{:T(128)} %convert_element_type.30, () %tuple.47, (bf16[1,4,24,512]{3,2,1,0:T(8,128)(2,1)S(1)}, bf16[8,512,512]{2,1,0:T(8,128)(2,1)}, f32[8,2,4]{2,1,0:T(2,128)S(1)}, f32[1,2,1,256]{3,1,2,0:T(2,128)S(1)}, f32[1,2,1,256]{3,1,2,0:T(2,128)S(1)}) %tuple.48), branch_computations={%region_1.1_spmd, %region_2.2_spmd} | conditional | flops 412459008 | bytes 26636324 | solution.py:81
  250.9 5.8 %collective-permute-done.2 = bf16[1,2,24,512]{3,1,2,0:T(2,128)(2,1)S(1)} collective-permute-done((bf16[1,2,24,512]{3,1,2,0:T(2,128)(2,1)S(1)}, bf16[1,2,24,512]{3,1,2,0:T(2,128)(2,1)S(1)}, u32[]{:S(2)}, u32[]{:S(2)}) %collective-permute-start.2) | collective-permute-done | bytes 49184 | tf_op jit(solution)/shard_map/while/body/eval_jaxpr/ppermute | solution.py:23
  263.6 11.0 %conditional.2 = (bf16[1,2,24,512]{3,1,2,0:T(2,128)(2,1)S(1)}) conditional(s32[]{:T(128)} %convert_element_type.30, () %tuple.47, (bf16[1,4,24,512]{3,2,1,0:T(8,128)(2,1)S(1)}, bf16[8,512,512]{2,1,0:T(8,128)(2,1)}, f32[8,2,4]{2,1,0:T(2,128)S(1)}, f32[1,2,1,256]{3,1,2,0:T(2,128)S(1)}, f32[1,2,1,256]{3,1,2,0:T(2,128)S(1)}) %tuple.48), branch_computations={%region_1.1_spmd, %region_2.2_spmd} | conditional | flops 412459008 | bytes 26636324 | solution.py:81
  (277 shorter events, 126.3 us)
Async XLA Ops:
  15.8 5.9 %collective-permute-start = (bf16[1,1,24,512]{3,2,1,0:T(8,128)(2,1)S(1)}, bf16[1,1,24,512]{3,2,1,0:T(8,128)(2,1)S(1)}, u32[]{:S(2)}, u32[]{:S(2)}) collective-permute-start(bf16[1,1,24,512]{3,2,1,0:T(8,128)(2,1)S(1)} %get-tuple-element.325), channel_id=1, source_target_pairs={{8,0},{16,8},{24,16},{9,1},{17,9},{25,17},{10,2},{18,10},{26,18},{... | collective-permute-start | bytes 73736 | tf_op jit(solution)/shard_map/while/body/eval_jaxpr/ppermute | solution.py:15
  17.1 5.5 %collective-permute-start.1 = (bf16[1,1,24,512]{3,2,1,0:T(8,128)(2,1)S(1)}, bf16[1,1,24,512]{3,2,1,0:T(8,128)(2,1)S(1)}, u32[]{:S(2)}, u32[]{:S(2)}) collective-permute-start(bf16[1,1,24,512]{3,2,1,0:T(8,128)(2,1)S(1)} %get-tuple-element.326), channel_id=1, source_target_pairs={{0,8},{8,16},{16,24},{1,9},{9,17},{17,25},{2,10},{10,18},{18,26},{... | collective-permute-start | bytes 73736 | tf_op jit(solution)/shard_map/while/body/eval_jaxpr/ppermute | solution.py:12
  22.7 6.3 %collective-permute-start.2 = (bf16[1,2,24,512]{3,1,2,0:T(2,128)(2,1)S(1)}, bf16[1,2,24,512]{3,1,2,0:T(2,128)(2,1)S(1)}, u32[]{:S(2)}, u32[]{:S(2)}) collective-permute-start(bf16[1,2,24,512]{3,1,2,0:T(2,128)(2,1)S(1)} %get-tuple-element.369), channel_id=1, source_target_pairs={{0,1},{1,2},{2,3},{3,4},{4,5},{5,6},{6,7},{8,9},{9,10},{10,11},{11... | collective-permute-start | bytes 147464 | tf_op jit(solution)/shard_map/while/body/eval_jaxpr/ppermute | solution.py:23
  29.0 5.9 %collective-permute-start = (bf16[1,1,24,512]{3,2,1,0:T(8,128)(2,1)S(1)}, bf16[1,1,24,512]{3,2,1,0:T(8,128)(2,1)S(1)}, u32[]{:S(2)}, u32[]{:S(2)}) collective-permute-start(bf16[1,1,24,512]{3,2,1,0:T(8,128)(2,1)S(1)} %get-tuple-element.325), channel_id=1, source_target_pairs={{8,0},{16,8},{24,16},{9,1},{17,9},{25,17},{10,2},{18,10},{26,18},{... | collective-permute-start | bytes 73736 | tf_op jit(solution)/shard_map/while/body/eval_jaxpr/ppermute | solution.py:15
  30.3 5.5 %collective-permute-start.1 = (bf16[1,1,24,512]{3,2,1,0:T(8,128)(2,1)S(1)}, bf16[1,1,24,512]{3,2,1,0:T(8,128)(2,1)S(1)}, u32[]{:S(2)}, u32[]{:S(2)}) collective-permute-start(bf16[1,1,24,512]{3,2,1,0:T(8,128)(2,1)S(1)} %get-tuple-element.326), channel_id=1, source_target_pairs={{0,8},{8,16},{16,24},{1,9},{9,17},{17,25},{2,10},{10,18},{18,26},{... | collective-permute-start | bytes 73736 | tf_op jit(solution)/shard_map/while/body/eval_jaxpr/ppermute | solution.py:12
  35.9 6.3 %collective-permute-start.2 = (bf16[1,2,24,512]{3,1,2,0:T(2,128)(2,1)S(1)}, bf16[1,2,24,512]{3,1,2,0:T(2,128)(2,1)S(1)}, u32[]{:S(2)}, u32[]{:S(2)}) collective-permute-start(bf16[1,2,24,512]{3,1,2,0:T(2,128)(2,1)S(1)} %get-tuple-element.369), channel_id=1, source_target_pairs={{0,1},{1,2},{2,3},{3,4},{4,5},{5,6},{6,7},{8,9},{9,10},{10,11},{11... | collective-permute-start | bytes 147464 | tf_op jit(solution)/shard_map/while/body/eval_jaxpr/ppermute | solution.py:23
  42.2 5.9 %collective-permute-start = (bf16[1,1,24,512]{3,2,1,0:T(8,128)(2,1)S(1)}, bf16[1,1,24,512]{3,2,1,0:T(8,128)(2,1)S(1)}, u32[]{:S(2)}, u32[]{:S(2)}) collective-permute-start(bf16[1,1,24,512]{3,2,1,0:T(8,128)(2,1)S(1)} %get-tuple-element.325), channel_id=1, source_target_pairs={{8,0},{16,8},{24,16},{9,1},{17,9},{25,17},{10,2},{18,10},{26,18},{... | collective-permute-start | bytes 73736 | tf_op jit(solution)/shard_map/while/body/eval_jaxpr/ppermute | solution.py:15
  43.5 5.5 %collective-permute-start.1 = (bf16[1,1,24,512]{3,2,1,0:T(8,128)(2,1)S(1)}, bf16[1,1,24,512]{3,2,1,0:T(8,128)(2,1)S(1)}, u32[]{:S(2)}, u32[]{:S(2)}) collective-permute-start(bf16[1,1,24,512]{3,2,1,0:T(8,128)(2,1)S(1)} %get-tuple-element.326), channel_id=1, source_target_pairs={{0,8},{8,16},{16,24},{1,9},{9,17},{17,25},{2,10},{10,18},{18,26},{... | collective-permute-start | bytes 73736 | tf_op jit(solution)/shard_map/while/body/eval_jaxpr/ppermute | solution.py:12
  49.1 6.3 %collective-permute-start.2 = (bf16[1,2,24,512]{3,1,2,0:T(2,128)(2,1)S(1)}, bf16[1,2,24,512]{3,1,2,0:T(2,128)(2,1)S(1)}, u32[]{:S(2)}, u32[]{:S(2)}) collective-permute-start(bf16[1,2,24,512]{3,1,2,0:T(2,128)(2,1)S(1)} %get-tuple-element.369), channel_id=1, source_target_pairs={{0,1},{1,2},{2,3},{3,4},{4,5},{5,6},{6,7},{8,9},{9,10},{10,11},{11... | collective-permute-start | bytes 147464 | tf_op jit(solution)/shard_map/while/body/eval_jaxpr/ppermute | solution.py:23
  55.4 5.9 %collective-permute-start = (bf16[1,1,24,512]{3,2,1,0:T(8,128)(2,1)S(1)}, bf16[1,1,24,512]{3,2,1,0:T(8,128)(2,1)S(1)}, u32[]{:S(2)}, u32[]{:S(2)}) collective-permute-start(bf16[1,1,24,512]{3,2,1,0:T(8,128)(2,1)S(1)} %get-tuple-element.325), channel_id=1, source_target_pairs={{8,0},{16,8},{24,16},{9,1},{17,9},{25,17},{10,2},{18,10},{26,18},{... | collective-permute-start | bytes 73736 | tf_op jit(solution)/shard_map/while/body/eval_jaxpr/ppermute | solution.py:15
  62.3 6.3 %collective-permute-start.2 = (bf16[1,2,24,512]{3,1,2,0:T(2,128)(2,1)S(1)}, bf16[1,2,24,512]{3,1,2,0:T(2,128)(2,1)S(1)}, u32[]{:S(2)}, u32[]{:S(2)}) collective-permute-start(bf16[1,2,24,512]{3,1,2,0:T(2,128)(2,1)S(1)} %get-tuple-element.369), channel_id=1, source_target_pairs={{0,1},{1,2},{2,3},{3,4},{4,5},{5,6},{6,7},{8,9},{9,10},{10,11},{11... | collective-permute-start | bytes 147464 | tf_op jit(solution)/shard_map/while/body/eval_jaxpr/ppermute | solution.py:23
  68.6 5.9 %collective-permute-start = (bf16[1,1,24,512]{3,2,1,0:T(8,128)(2,1)S(1)}, bf16[1,1,24,512]{3,2,1,0:T(8,128)(2,1)S(1)}, u32[]{:S(2)}, u32[]{:S(2)}) collective-permute-start(bf16[1,1,24,512]{3,2,1,0:T(8,128)(2,1)S(1)} %get-tuple-element.325), channel_id=1, source_target_pairs={{8,0},{16,8},{24,16},{9,1},{17,9},{25,17},{10,2},{18,10},{26,18},{... | collective-permute-start | bytes 73736 | tf_op jit(solution)/shard_map/while/body/eval_jaxpr/ppermute | solution.py:15
  75.5 6.3 %collective-permute-start.2 = (bf16[1,2,24,512]{3,1,2,0:T(2,128)(2,1)S(1)}, bf16[1,2,24,512]{3,1,2,0:T(2,128)(2,1)S(1)}, u32[]{:S(2)}, u32[]{:S(2)}) collective-permute-start(bf16[1,2,24,512]{3,1,2,0:T(2,128)(2,1)S(1)} %get-tuple-element.369), channel_id=1, source_target_pairs={{0,1},{1,2},{2,3},{3,4},{4,5},{5,6},{6,7},{8,9},{9,10},{10,11},{11... | collective-permute-start | bytes 147464 | tf_op jit(solution)/shard_map/while/body/eval_jaxpr/ppermute | solution.py:23
  81.9 5.9 %collective-permute-start = (bf16[1,1,24,512]{3,2,1,0:T(8,128)(2,1)S(1)}, bf16[1,1,24,512]{3,2,1,0:T(8,128)(2,1)S(1)}, u32[]{:S(2)}, u32[]{:S(2)}) collective-permute-start(bf16[1,1,24,512]{3,2,1,0:T(8,128)(2,1)S(1)} %get-tuple-element.325), channel_id=1, source_target_pairs={{8,0},{16,8},{24,16},{9,1},{17,9},{25,17},{10,2},{18,10},{26,18},{... | collective-permute-start | bytes 73736 | tf_op jit(solution)/shard_map/while/body/eval_jaxpr/ppermute | solution.py:15
  88.7 67.7 %collective-permute-start.2 = (bf16[1,2,24,512]{3,1,2,0:T(2,128)(2,1)S(1)}, bf16[1,2,24,512]{3,1,2,0:T(2,128)(2,1)S(1)}, u32[]{:S(2)}, u32[]{:S(2)}) collective-permute-start(bf16[1,2,24,512]{3,1,2,0:T(2,128)(2,1)S(1)} %get-tuple-element.369), channel_id=1, source_target_pairs={{0,1},{1,2},{2,3},{3,4},{4,5},{5,6},{6,7},{8,9},{9,10},{10,11},{11... | collective-permute-start | bytes 147464 | tf_op jit(solution)/shard_map/while/body/eval_jaxpr/ppermute | solution.py:23
  156.5 5.9 %collective-permute-start = (bf16[1,1,24,512]{3,2,1,0:T(8,128)(2,1)S(1)}, bf16[1,1,24,512]{3,2,1,0:T(8,128)(2,1)S(1)}, u32[]{:S(2)}, u32[]{:S(2)}) collective-permute-start(bf16[1,1,24,512]{3,2,1,0:T(8,128)(2,1)S(1)} %get-tuple-element.325), channel_id=1, source_target_pairs={{8,0},{16,8},{24,16},{9,1},{17,9},{25,17},{10,2},{18,10},{26,18},{... | collective-permute-start | bytes 73736 | tf_op jit(solution)/shard_map/while/body/eval_jaxpr/ppermute | solution.py:15
  174.3 7.2 %collective-permute-start.2 = (bf16[1,2,24,512]{3,1,2,0:T(2,128)(2,1)S(1)}, bf16[1,2,24,512]{3,1,2,0:T(2,128)(2,1)S(1)}, u32[]{:S(2)}, u32[]{:S(2)}) collective-permute-start(bf16[1,2,24,512]{3,1,2,0:T(2,128)(2,1)S(1)} %get-tuple-element.369), channel_id=1, source_target_pairs={{0,1},{1,2},{2,3},{3,4},{4,5},{5,6},{6,7},{8,9},{9,10},{10,11},{11... | collective-permute-start | bytes 147464 | tf_op jit(solution)/shard_map/while/body/eval_jaxpr/ppermute | solution.py:23
  181.6 5.9 %collective-permute-start = (bf16[1,1,24,512]{3,2,1,0:T(8,128)(2,1)S(1)}, bf16[1,1,24,512]{3,2,1,0:T(8,128)(2,1)S(1)}, u32[]{:S(2)}, u32[]{:S(2)}) collective-permute-start(bf16[1,1,24,512]{3,2,1,0:T(8,128)(2,1)S(1)} %get-tuple-element.325), channel_id=1, source_target_pairs={{8,0},{16,8},{24,16},{9,1},{17,9},{25,17},{10,2},{18,10},{26,18},{... | collective-permute-start | bytes 73736 | tf_op jit(solution)/shard_map/while/body/eval_jaxpr/ppermute | solution.py:15
  199.4 7.2 %collective-permute-start.2 = (bf16[1,2,24,512]{3,1,2,0:T(2,128)(2,1)S(1)}, bf16[1,2,24,512]{3,1,2,0:T(2,128)(2,1)S(1)}, u32[]{:S(2)}, u32[]{:S(2)}) collective-permute-start(bf16[1,2,24,512]{3,1,2,0:T(2,128)(2,1)S(1)} %get-tuple-element.369), channel_id=1, source_target_pairs={{0,1},{1,2},{2,3},{3,4},{4,5},{5,6},{6,7},{8,9},{9,10},{10,11},{11... | collective-permute-start | bytes 147464 | tf_op jit(solution)/shard_map/while/body/eval_jaxpr/ppermute | solution.py:23
  206.7 5.9 %collective-permute-start = (bf16[1,1,24,512]{3,2,1,0:T(8,128)(2,1)S(1)}, bf16[1,1,24,512]{3,2,1,0:T(8,128)(2,1)S(1)}, u32[]{:S(2)}, u32[]{:S(2)}) collective-permute-start(bf16[1,1,24,512]{3,2,1,0:T(8,128)(2,1)S(1)} %get-tuple-element.325), channel_id=1, source_target_pairs={{8,0},{16,8},{24,16},{9,1},{17,9},{25,17},{10,2},{18,10},{26,18},{... | collective-permute-start | bytes 73736 | tf_op jit(solution)/shard_map/while/body/eval_jaxpr/ppermute | solution.py:15
  224.5 7.2 %collective-permute-start.2 = (bf16[1,2,24,512]{3,1,2,0:T(2,128)(2,1)S(1)}, bf16[1,2,24,512]{3,1,2,0:T(2,128)(2,1)S(1)}, u32[]{:S(2)}, u32[]{:S(2)}) collective-permute-start(bf16[1,2,24,512]{3,1,2,0:T(2,128)(2,1)S(1)} %get-tuple-element.369), channel_id=1, source_target_pairs={{0,1},{1,2},{2,3},{3,4},{4,5},{5,6},{6,7},{8,9},{9,10},{10,11},{11... | collective-permute-start | bytes 147464 | tf_op jit(solution)/shard_map/while/body/eval_jaxpr/ppermute | solution.py:23
  231.7 5.9 %collective-permute-start = (bf16[1,1,24,512]{3,2,1,0:T(8,128)(2,1)S(1)}, bf16[1,1,24,512]{3,2,1,0:T(8,128)(2,1)S(1)}, u32[]{:S(2)}, u32[]{:S(2)}) collective-permute-start(bf16[1,1,24,512]{3,2,1,0:T(8,128)(2,1)S(1)} %get-tuple-element.325), channel_id=1, source_target_pairs={{8,0},{16,8},{24,16},{9,1},{17,9},{25,17},{10,2},{18,10},{26,18},{... | collective-permute-start | bytes 73736 | tf_op jit(solution)/shard_map/while/body/eval_jaxpr/ppermute | solution.py:15
  249.5 7.2 %collective-permute-start.2 = (bf16[1,2,24,512]{3,1,2,0:T(2,128)(2,1)S(1)}, bf16[1,2,24,512]{3,1,2,0:T(2,128)(2,1)S(1)}, u32[]{:S(2)}, u32[]{:S(2)}) collective-permute-start(bf16[1,2,24,512]{3,1,2,0:T(2,128)(2,1)S(1)} %get-tuple-element.369), channel_id=1, source_target_pairs={{0,1},{1,2},{2,3},{3,4},{4,5},{5,6},{6,7},{8,9},{9,10},{10,11},{11... | collective-permute-start | bytes 147464 | tf_op jit(solution)/shard_map/while/body/eval_jaxpr/ppermute | solution.py:23
  256.8 5.9 %collective-permute-start = (bf16[1,1,24,512]{3,2,1,0:T(8,128)(2,1)S(1)}, bf16[1,1,24,512]{3,2,1,0:T(8,128)(2,1)S(1)}, u32[]{:S(2)}, u32[]{:S(2)}) collective-permute-start(bf16[1,1,24,512]{3,2,1,0:T(8,128)(2,1)S(1)} %get-tuple-element.325), channel_id=1, source_target_pairs={{8,0},{16,8},{24,16},{9,1},{17,9},{25,17},{10,2},{18,10},{26,18},{... | collective-permute-start | bytes 73736 | tf_op jit(solution)/shard_map/while/body/eval_jaxpr/ppermute | solution.py:15
  (23 other events, 112.5 us)
where the time goes:
time: 281 us; the launch traced here: 278 us
  waiting for transfers between devices  129 us (46%)
  starting transfers between devices  85.1 us (30%)
  matrix products  54 us (19%)
  other arithmetic  3.95 us (1%)
  local copies, waits for them, and re-layouts  3.89 us (1%)
    ppermute x12, waiting for transfers between devices, shifted(): return lax.ppermute(array, axis, pairs)  119 us
    ppermute x12, starting transfers between devices, with_halo(): lax.ppermute(lax.slice_in_dim(block, block.shape[dim] - width, None, axis...  54.1 us
    dot_general x40, matrix products, advance(): jnp.dot(flat_rows, blocks[entry], preferred_element_type=jnp.float32)  30.4 us
    dot_general x40, matrix products, advance(): jnp.einsum('wj,bjsd->bwsd', selection[entry], product, precision=lax.Prec...  23.4 us
    ppermute x12, starting transfers between devices, with_halo(): lax.ppermute(lax.slice_in_dim(block, 0, width, axis=dim), axis, backward)  15.5 us
    ppermute x12, starting transfers between devices, shifted(): return lax.ppermute(array, axis, pairs)  15.5 us
    ppermute x12, waiting for transfers between devices, with_halo(): lax.ppermute(lax.slice_in_dim(block, block.shape[dim] - width, None, axis...  10.6 us
  transfers between devices with their start and end apart: 36, of which 24 were waited for; matrix products, arithmetic and copies ran while one was open for 0% of the time, Pallas kernels for 0%

commit v1 on v0

v1 whole, which is shorter than its diff:
```python
import functools

import jax
import jax.numpy as jnp
from jax import lax
from jax.experimental import pallas as pl
from jax.experimental.pallas import tpu as pltpu
from jax.sharding import PartitionSpec as P

MESH = pl.DeviceIdType.MESH


def kernel(
    wins, secs, links, kinds, counts, screen, initial, props, out,
    inbox, table, mixed, coef, turn, table_sem, seed_sem, send_sem, recv_sem,
):
    z = lax.axis_index("win")
    s = lax.axis_index("sec")
    fronts, local, sources, width = initial.shape
    coeffs = width // 2
    entries = props.shape[0] // width
    length = links.shape[2]
    has_low = z > 0
    has_high = z < wins - 1
    first = s == 0
    sends = s < secs - 1

    load_table = pltpu.make_async_copy(props, table, table_sem)
    load_table.start()

    barrier = pltpu.get_barrier_semaphore()

    def greet(win, sec):
        pl.semaphore_signal(barrier, inc=1, device_id=(win, sec), device_id_type=MESH)

    @pl.when(s > 0)
    def _():
        greet(z, s - 1)

    @pl.when(has_low)
    def _():
        greet(z - 1, jnp.maximum(s - 1, 0))

    @pl.when(has_high)
    def _():
        greet(z + 1, jnp.maximum(s - 1, 0))

    sides = has_low.astype(jnp.int32) + has_high.astype(jnp.int32)
    expected = jnp.where(sends, 1 + sides, 0) + jnp.where(first, sides, 0)

    @pl.when(expected > 0)
    def _():
        pl.semaphore_wait(barrier, expected)

    def remote(source, target, send, receive, win, sec):
        return pltpu.make_async_remote_copy(
            src_ref=source, dst_ref=target, send_sem=send, recv_sem=receive,
            device_id=(win, sec), device_id_type=MESH,
        )

    def seed_own(f):
        return pltpu.make_async_copy(
            initial.at[f], inbox.at[f, pl.ds(1, local)], recv_sem.at[f, 0]
        )

    def seed_low(f):
        return remote(
            initial.at[f, 0], inbox.at[f, local + 1], seed_sem.at[f, 0], recv_sem.at[f, 2], z - 1, s
        )

    def seed_high(f):
        return remote(
            initial.at[f, local - 1], inbox.at[f, 0], seed_sem.at[f, 1], recv_sem.at[f, 1], z + 1, s
        )

    @pl.when(first & has_low)
    def _():
        for f in range(fronts):
            seed_low(f).start()

    @pl.when(first & has_high)
    def _():
        for f in range(fronts):
            seed_high(f).start()

    @pl.when(first)
    def _():
        for f in range(fronts):
            seed_own(f).start()

    @pl.when(jnp.logical_not(has_low))
    def _():
        inbox[:, 0] = jnp.zeros((fronts, sources, width), jnp.bfloat16)

    @pl.when(jnp.logical_not(has_high))
    def _():
        inbox[:, local + 1] = jnp.zeros((fronts, sources, width), jnp.bfloat16)

    for w in range(local):
        live = counts[0, w]
        codes = []
        for l in range(length):
            offset = links[0, w, l] - (z * local + w - 1)
            codes.append(jnp.where(l < live, kinds[0, w, l] * 3 + offset, -1))
        for code in range(entries * 3):
            hits = sum((c == code).astype(jnp.int32) for c in codes)
            coef[w, code] = hits.astype(jnp.float32)
        scale = lax.rsqrt(jnp.full((1, coeffs), live, jnp.int32).astype(jnp.float32))
        phase = screen[0, pl.ds(w, 1), :]
        turn[w, 0] = jnp.broadcast_to(jnp.cos(phase) * scale, turn.shape[2:])
        turn[w, 1] = jnp.broadcast_to(jnp.sin(phase) * scale, turn.shape[2:])

    load_table.wait()

    def send_own(f):
        return remote(
            out.at[0, f], inbox.at[f, pl.ds(1, local)], send_sem.at[f, 0], recv_sem.at[f, 0], z, s + 1
        )

    def send_low(f):
        return remote(
            out.at[0, f, 0], inbox.at[f, local + 1], send_sem.at[f, 1], recv_sem.at[f, 2], z - 1, s + 1
        )

    def send_high(f):
        return remote(
            out.at[0, f, local - 1], inbox.at[f, 0], send_sem.at[f, 2], recv_sem.at[f, 1], z + 1, s + 1
        )

    def arrived(ref, sem):
        pltpu.make_async_copy(ref, ref, sem).wait()

    half = entries * width // 2

    def step(f, carry):
        arrived(inbox.at[f, pl.ds(1, local)], recv_sem.at[f, 0])

        @pl.when(has_low)
        def _():
            arrived(inbox.at[f, 0], recv_sem.at[f, 1])

        @pl.when(has_high)
        def _():
            arrived(inbox.at[f, local + 1], recv_sem.at[f, 2])

        held = [inbox[f, j].astype(jnp.float32) for j in range(local + 2)]
        for entry in range(entries):
            straight, crossed = [], []
            for w in range(local):
                total = coef[w, entry * 3] * held[w]
                for d in (1, 2):
                    total = total + coef[w, entry * 3 + d] * held[w + d]
                a, b = total[:, :coeffs], total[:, coeffs:]
                straight += [a, b]
                crossed += [-b, a]
            left = entry * width
            mixed[:, left : left + coeffs] = jnp.concatenate(straight, 0).astype(jnp.bfloat16)
            mixed[:, left + coeffs : left + width] = jnp.concatenate(crossed, 0).astype(jnp.bfloat16)
        total = jnp.dot(
            mixed[:, :half], table[:half], preferred_element_type=jnp.float32
        ) + jnp.dot(mixed[:, half:], table[half:], preferred_element_type=jnp.float32)
        for w in range(local):
            top = 2 * w * sources
            a = total[top : top + sources]
            b = total[top + sources : top + 2 * sources]
            c = turn[w, 0, :1]
            d = turn[w, 1, :1]
            out[0, f, w, :, :coeffs] = (a * c - b * d).astype(jnp.bfloat16)
            out[0, f, w, :, coeffs:] = (a * d + b * c).astype(jnp.bfloat16)

        @pl.when(sends & has_low)
        def _():
            send_low(f).start()

        @pl.when(sends & has_high)
        def _():
            send_high(f).start()

        @pl.when(sends)
        def _():
            send_own(f).start()

        return carry

    lax.fori_loop(0, fronts, step, 0)

    @pl.when(first & has_low)
    def _():
        for f in range(fronts):
            seed_low(f).wait_send()

    @pl.when(first & has_high)
    def _():
        for f in range(fronts):
            seed_high(f).wait_send()

    @pl.when(sends & has_low)
    def _():
        for f in range(fronts):
            send_low(f).wait_send()

    @pl.when(sends & has_high)
    def _():
        for f in range(fronts):
            send_high(f).wait_send()

    @pl.when(sends)
    def _():
        for f in range(fronts):
            send_own(f).wait_send()


def solution(mesh):
    wins, secs = mesh.shape["win"], mesh.shape["sec"]

    def run(initial, props, screen, links, kinds, counts):
        fronts, local, sources, width = initial.shape
        coeffs = width // 2
        entries = props.shape[1]
        smem = pl.BlockSpec(memory_space=pltpu.SMEM)
        vmem = pl.BlockSpec(memory_space=pltpu.VMEM)
        whole = pl.BlockSpec(memory_space=pl.ANY)
        return pl.pallas_call(
            functools.partial(kernel, wins, secs),
            out_shape=jax.ShapeDtypeStruct((1, fronts, local, sources, width), jnp.bfloat16),
            in_specs=[smem, smem, smem, vmem, whole, whole],
            out_specs=vmem,
            scratch_shapes=[
                pltpu.VMEM((fronts, local + 2, sources, width), jnp.bfloat16),
                pltpu.VMEM((entries * width, coeffs), jnp.bfloat16),
                pltpu.VMEM((2 * local * sources, entries * width), jnp.bfloat16),
                pltpu.SMEM((local, 3 * entries), jnp.float32),
                pltpu.VMEM((local, 2, 8, coeffs), jnp.float32),
                pltpu.SemaphoreType.DMA,
                pltpu.SemaphoreType.DMA((fronts, 2)),
                pltpu.SemaphoreType.DMA((fronts, 3)),
                pltpu.SemaphoreType.DMA((fronts, 3)),
            ],
            compiler_params=pltpu.CompilerParams(collective_id=0, has_side_effects=True),
            name="beamlets",
        )(links, kinds, counts, screen, initial, props.reshape(entries * width, coeffs))

    placed = (
        P(None, "win", None, None),
        P("sec", None, None, None, None),
        P("sec", "win", None),
        P("sec", "win", None),
        P("sec", "win", None),
        P("sec", "win"),
    )
    return jax.shard_map(
        run,
        mesh=mesh,
        in_specs=placed,
        out_specs=P("sec", None, "win", None, None),
        check_vma=False,
    )
```

time: 281 us -> 38.8 us (0.14)
  waiting for transfers between devices: 129 us -> 0 us
  starting transfers between devices: 85.1 us -> 0 us
  matrix products: 54 us -> 0 us
  Pallas kernels: 0 us -> 36.9 us
  other arithmetic: 3.95 us -> 0 us
    ppermute x36 -> x0, waiting for transfers between devices: 129 us -> none  [the longest x12 119 us: shifted(): return lax.ppermute(array, axis, pairs)]
    ppermute x36 -> x0, starting transfers between devices: 85.1 us -> none  [the longest x12 54.1 us: with_halo(): lax.ppermute(lax.slice_in_dim(block, block.shape[dim] - width, None, axis...]
    dot_general x81 -> x0, matrix products: 54 us -> none  [the longest x40 30.4 us: advance(): jnp.dot(flat_rows, blocks[entry], preferred_element_type=jnp.float32)]
    pallas_call x0 -> x1, Pallas kernels: none -> 36.9 us  [run(): pl.pallas_call(functools.partial(kernel, wins, secs), out_shape=jax.Shape...]
  transfers between devices with their start and end apart: 36 -> 0, of which waited for: 24 -> 0; matrix products, arithmetic and copies ran while one was open for 0% -> 0% of each run, Pallas kernels for 0% -> 0%
where the time goes in v1:
time: 38.8 us; the launch traced here: 38.6 us
  Pallas kernels  36.9 us (95%)
  local copies, waits for them, and re-layouts  1.65 us (4%)
    pallas_call x1, Pallas kernels, run(): pl.pallas_call(functools.partial(kernel, wins, secs), out_shape=jax.Shape...  36.9 us
    unnamed x1, local copies, waits for them, and re-layouts  1.65 us

profile of v1, /device:TPU:7, one launch (start us, length us, event | category | flops | bytes accessed | tf_op | source)
XLA Modules:
  0.0 38.6 jit_solution(7345097065431341266)
XLA Ops:
  0.0 36.9 %beamlets.1 = bf16[1,5,2,24,512]{4,3,2,1,0:T(8,128)(2,1)} custom-call(s32[1,2,6]{2,1,0:T(2,128)} %links.1, s32[1,2,6]{2,1,0:T(2,128)} %kinds.1, s32[1,2]{1,0:T(1,128)} %counts.1, f32[1,2,256]{2,1,0:T(2,128)} %screen.1, bf16[5,2,24,512]{3,2,1,0:T(8,128)(2,1)} %initial.1, bf16[4096,256]{1,0:T(8,128)(2,1)} %bitcast.1), custom_call_target="tpu_custom_call" | custom-call | tf_op jit(solution)/shard_map/beamlets/pallas_call | solution.py:223
  36.9 1.7 %copy.8 = bf16[1,5,2,24,512]{4,3,2,1,0:T(8,128)(2,1)} copy(bf16[1,5,2,24,512]{4,3,2,1,0:T(8,128)(2,1)} %beamlets.1) | data formatting | bytes 491520

commit v2 on v1

--- a/solution.py
+++ b/solution.py
@@ -18,15 +18,19 @@
     s = lax.axis_index("sec")
     fronts, local, sources, width = initial.shape
     coeffs = width // 2
-    entries = props.shape[0] // width
+    entries = props.shape[0]
     length = links.shape[2]
     has_low = z > 0
     has_high = z < wins - 1
     first = s == 0
     sends = s < secs - 1
 
-    load_table = pltpu.make_async_copy(props, table, table_sem)
-    load_table.start()
+    loads = [
+        pltpu.make_async_copy(props.at[:, part], table.at[part], table_sem.at[part])
+        for part in (0, 1)
+    ]
+    for load in loads:
+        load.start()
 
     barrier = pltpu.get_barrier_semaphore()
 
@@ -110,7 +114,8 @@
         turn[w, 0] = jnp.broadcast_to(jnp.cos(phase) * scale, turn.shape[2:])
         turn[w, 1] = jnp.broadcast_to(jnp.sin(phase) * scale, turn.shape[2:])
 
-    load_table.wait()
+    for load in loads:
+        load.wait()
 
     def send_own(f):
         return remote(
@@ -130,7 +135,7 @@
     def arrived(ref, sem):
         pltpu.make_async_copy(ref, ref, sem).wait()
 
-    half = entries * width // 2
+    depth = entries * coeffs
 
     def step(f, carry):
         arrived(inbox.at[f, pl.ds(1, local)], recv_sem.at[f, 0])
@@ -145,29 +150,44 @@
 
         held = [inbox[f, j].astype(jnp.float32) for j in range(local + 2)]
         for entry in range(entries):
-            straight, crossed = [], []
+            stack = []
             for w in range(local):
                 total = coef[w, entry * 3] * held[w]
                 for d in (1, 2):
                     total = total + coef[w, entry * 3 + d] * held[w + d]
                 a, b = total[:, :coeffs], total[:, coeffs:]
-                straight += [a, b]
-                crossed += [-b, a]
-            left = entry * width
-            mixed[:, left : left + coeffs] = jnp.concatenate(straight, 0).astype(jnp.bfloat16)
-            mixed[:, left + coeffs : left + width] = jnp.concatenate(crossed, 0).astype(jnp.bfloat16)
-        total = jnp.dot(
-            mixed[:, :half], table[:half], preferred_element_type=jnp.float32
-        ) + jnp.dot(mixed[:, half:], table[half:], preferred_element_type=jnp.float32)
+                stack += [a, b]
+            left = entry * coeffs
+            mixed[:, left : left + coeffs] = jnp.concatenate(stack, 0).astype(jnp.bfloat16)
+        lhs = mixed[...]
+        by_real, by_imag = (
+            jnp.dot(lhs, table[part].reshape(depth, coeffs), preferred_element_type=jnp.float32)
+            for part in (0, 1)
+        )
         for w in range(local):
             top = 2 * w * sources
-            a = total[top : top + sources]
-            b = total[top + sources : top + 2 * sources]
+            mid, low = top + sources, top + 2 * sources
+            a = by_real[top:mid] - by_imag[mid:low]
+            b = by_real[mid:low] + by_imag[top:mid]
             c = turn[w, 0, :1]
             d = turn[w, 1, :1]
             out[0, f, w, :, :coeffs] = (a * c - b * d).astype(jnp.bfloat16)
             out[0, f, w, :, coeffs:] = (a * d + b * c).astype(jnp.bfloat16)
 
+        @pl.when(f >= 2)
+        def _():
+            @pl.when(sends & has_low)
+            def _():
+                send_low(f - 2).wait_send()
+
+            @pl.when(sends & has_high)
+            def _():
+                send_high(f - 2).wait_send()
+
+            @pl.when(sends)
+            def _():
+                send_own(f - 2).wait_send()
+
         @pl.when(sends & has_low)
         def _():
             send_low(f).start()
@@ -196,17 +216,17 @@
 
     @pl.when(sends & has_low)
     def _():
-        for f in range(fronts):
+        for f in range(max(fronts - 2, 0), fronts):
             send_low(f).wait_send()
 
     @pl.when(sends & has_high)
     def _():
-        for f in range(fronts):
+        for f in range(max(fronts - 2, 0), fronts):
             send_high(f).wait_send()
 
     @pl.when(sends)
     def _():
-        for f in range(fronts):
+        for f in range(max(fronts - 2, 0), fronts):
             send_own(f).wait_send()
 
 
@@ -227,18 +247,18 @@
             out_specs=vmem,
             scratch_shapes=[
                 pltpu.VMEM((fronts, local + 2, sources, width), jnp.bfloat16),
-                pltpu.VMEM((entries * width, coeffs), jnp.bfloat16),
-                pltpu.VMEM((2 * local * sources, entries * width), jnp.bfloat16),
+                pltpu.VMEM((2, entries, coeffs, coeffs), jnp.bfloat16),
+                pltpu.VMEM((2 * local * sources, entries * coeffs), jnp.bfloat16),
                 pltpu.SMEM((local, 3 * entries), jnp.float32),
                 pltpu.VMEM((local, 2, 8, coeffs), jnp.float32),
-                pltpu.SemaphoreType.DMA,
+                pltpu.SemaphoreType.DMA((2,)),
                 pltpu.SemaphoreType.DMA((fronts, 2)),
                 pltpu.SemaphoreType.DMA((fronts, 3)),
                 pltpu.SemaphoreType.DMA((fronts, 3)),
             ],
             compiler_params=pltpu.CompilerParams(collective_id=0, has_side_effects=True),
             name="beamlets",
-        )(links, kinds, counts, screen, initial, props.reshape(entries * width, coeffs))
+        )(links, kinds, counts, screen, initial, props[0])
 
     placed = (
         P(None, "win", None, None),

time: 38.8 us -> 38.1 us (0.982)
  Pallas kernels: 36.9 us -> 36.3 us
    pallas_call x1, Pallas kernels: 36.9 us -> 36.3 us  [run(): pl.pallas_call(functools.partial(kernel, wins, secs), out_shape=jax.Shape...]
where the time goes in v2:
time: 38.1 us; the launch traced here: 37.9 us
  Pallas kernels  36.3 us (95%)
  local copies, waits for them, and re-layouts  1.65 us (4%)
    pallas_call x1, Pallas kernels, run(): pl.pallas_call(functools.partial(kernel, wins, secs), out_shape=jax.Shape...  36.3 us
    unnamed x1, local copies, waits for them, and re-layouts  1.65 us

profile of v2, /device:TPU:7, one launch (start us, length us, event | category | flops | bytes accessed | tf_op | source)
XLA Modules:
  0.0 37.9 jit_solution(8895750778656101187)
XLA Ops:
  0.0 36.3 %beamlets.1 = bf16[1,5,2,24,512]{4,3,2,1,0:T(8,128)(2,1)} custom-call(s32[1,2,6]{2,1,0:T(2,128)} %links.1, s32[1,2,6]{2,1,0:T(2,128)} %kinds.1, s32[1,2]{1,0:T(1,128)} %counts.1, f32[1,2,256]{2,1,0:T(2,128)} %screen.1, bf16[5,2,24,512]{3,2,1,0:T(8,128)(2,1)} %initial.1, bf16[8,2,256,256]{3,2,1,0:T(8,128)(2,1)} %bitcast.1), custom_call_target="tpu_custom_call" | custom-call | tf_op jit(solution)/shard_map/beamlets/pallas_call | solution.py:243
  36.3 1.7 %copy.8 = bf16[1,5,2,24,512]{4,3,2,1,0:T(8,128)(2,1)} copy(bf16[1,5,2,24,512]{4,3,2,1,0:T(8,128)(2,1)} %beamlets.1) | data formatting | bytes 491520

commit v3 on v2

--- a/solution.py
+++ b/solution.py
@@ -242,7 +242,7 @@
         whole = pl.BlockSpec(memory_space=pl.ANY)
         return pl.pallas_call(
             functools.partial(kernel, wins, secs),
-            out_shape=jax.ShapeDtypeStruct((1, fronts, local, sources, width), jnp.bfloat16),
+            out_shape=pltpu.VMEM((1, fronts, local, sources, width), jnp.bfloat16),
             in_specs=[smem, smem, smem, vmem, whole, whole],
             out_specs=vmem,
             scratch_shapes=[

time: 38.1 us -> 36.5 us (0.958)
  local copies, waits for them, and re-layouts: 1.65 us -> 0.7 us
  Pallas kernels: 36.3 us -> 35.6 us
    unnamed x1, local copies, waits for them, and re-layouts: 1.65 us -> 0.7 us
    pallas_call x1, Pallas kernels: 36.3 us -> 35.6 us  [run(): pl.pallas_call(functools.partial(kernel, wins, secs), out_shape=pltpu.VME...]
where the time goes in v3:
time: 36.5 us; the launch traced here: 36.3 us
  Pallas kernels  35.6 us (98%)
  local copies, waits for them, and re-layouts  0.7 us (2%)
    pallas_call x1, Pallas kernels, run(): pl.pallas_call(functools.partial(kernel, wins, secs), out_shape=pltpu.VME...  35.6 us

profile of v3, /device:TPU:7, one launch (start us, length us, event | category | flops | bytes accessed | tf_op | source)
XLA Modules:
  0.0 36.3 jit_solution(8587860152720736565)
XLA Ops:
  0.0 35.6 %beamlets.1 = bf16[1,5,2,24,512]{4,3,2,1,0:T(8,128)(2,1)S(1)} custom-call(s32[1,2,6]{2,1,0:T(2,128)} %links.1, s32[1,2,6]{2,1,0:T(2,128)} %kinds.1, s32[1,2]{1,0:T(1,128)} %counts.1, f32[1,2,256]{2,1,0:T(2,128)} %screen.1, bf16[5,2,24,512]{3,2,1,0:T(8,128)(2,1)} %initial.1, bf16[8,2,256,256]{3,2,1,0:T(8,128)(2,1)} %bitcast.1), custom_call_target="tpu_custom_call" | custom-call | tf_op jit(solution)/shard_map/beamlets/pallas_call | solution.py:243
  35.6 0.7 %copy.8 = bf16[1,5,2,24,512]{4,3,2,1,0:T(8,128)(2,1)} copy(bf16[1,5,2,24,512]{4,3,2,1,0:T(8,128)(2,1)S(1)} %beamlets.1) | data formatting | bytes 491520
